TPU v7x, 32 devices: a whole 2x2x4 slice. The times are simulated.
32 devices in a mesh: dp: 4 (over y, x), space: 8 (over z, core).
Axes of the slice: x: 2, y: 2, z: 4, core: 2. Of those that a mesh axis runs over, the one named last changes fastest.
Arguments:
- volumes: bfloat16 [4, 4, 64, 32, 512], P('dp', None, 'space'), may hold values from -6 to 6
- first_kernel: bfloat16 [3, 3, 3, 4, 32], replicated, may hold values from -0.625 to 0.625
- second_kernel: float32 [3, 3, 3, 32, 64], replicated, may hold values from -0.21875 to 0.21875
- cotangent: bfloat16 [4, 64, 16, 8, 128], P('dp', None, 'space'), may hold values from -0.5 to 0.5
- first_moment: float32 [55296], P(('dp', 'space')), may hold values from -0.75 to 0.75
- second_moment: float32 [55296], P(('dp', 'space')), may hold values from 0.001 to 0.01
Outputs:
- activations: bfloat16 [4, 64, 16, 8, 128], P('dp', None, 'space')
- first_gradient: float32 [3, 3, 3, 4, 32], replicated
- new_kernel: float32 [3, 3, 3, 32, 64], replicated
- new_first_moment: float32 [55296], P(('dp', 'space'))
- new_second_moment: float32 [55296], P(('dp', 'space'))
All inputs are finite; a program needn't handle non-finite values.
Results may differ from a plain program's by a relative error of at most 0.0055.
The roundings to bfloat16 on the way count: a program that leaves them out, or rounds other values in their place, can miss the bound.
Values may be sent and summed in bfloat16 or wider, within the bound.
No kernel may reach another device: no remote copies, remote signals or barrier semaphores. Data moves between devices by JAX's collectives and lax.ppermute only.
A program may use at most 256 MiB of HBM per device.

v0:
```python
import jax
import jax.numpy as jnp
from jax import lax
from jax.sharding import PartitionSpec as P

SLOPE = 0.3
BETA_FIRST = 0.9
BETA_SECOND = 0.999
LEARN_RATE = 0.001
EPSILON = 1e-08
NUMBERS = ("NCDHW", "DHWIO", "NCDHW")


def from_behind(value, axis, steps):
    count = lax.axis_size(axis)
    first, last = (max(0, -steps), min(count, count - steps))
    return lax.ppermute(value, axis, [(source, source + steps) for source in range(first, last)])


def strided(inputs, kernel):
    return lax.conv_general_dilated(
        inputs,
        kernel,
        (2, 2, 2),
        [(0, 0), (1, 1), (1, 1)],
        dimension_numbers=NUMBERS,
        preferred_element_type=jnp.float32,
    )


def strided_exact(inputs, kernel, depth_pad):
    return lax.conv_general_dilated(
        inputs,
        kernel,
        (2, 2, 2),
        [depth_pad, (1, 1), (1, 1)],
        dimension_numbers=NUMBERS,
        preferred_element_type=jnp.float32,
    )


def leaky(values):
    return jnp.where(values > 0, values, SLOPE * values)


def leaky_slope(values):
    return jnp.where(values > 0, jnp.float32(1.0), jnp.float32(SLOPE))


def shards(volumes, first_kernel, second_kernel, cotangent, first_moment, second_moment):
    lower_plane = from_behind(volumes[:, :, -1:], "space", 1)
    padded_in = jnp.concatenate([lower_plane, volumes], axis=2)
    preact_one = strided(padded_in, first_kernel)
    hidden = leaky(preact_one).astype(jnp.bfloat16)
    lower_hidden = from_behind(hidden[:, :, -1:], "space", 1)
    padded_hidden = jnp.concatenate([lower_hidden, hidden], axis=2)
    kernel_half = second_kernel.astype(jnp.bfloat16)
    preact_two = strided(padded_hidden, kernel_half)
    activations = leaky(preact_two).astype(jnp.bfloat16)
    delta_two = (cotangent.astype(jnp.float32) * leaky_slope(preact_two)).astype(jnp.bfloat16)
    second_wide = kernel_half.astype(jnp.float32)
    hidden_wide = padded_hidden.astype(jnp.float32)
    delta_wide = delta_two.astype(jnp.float32)

    def second_map(activ, kernel):
        return strided_exact(activ, kernel, (0, 0))

    _, pull_second = jax.vjp(second_map, hidden_wide, second_wide)
    grad_padded, second_gradient = pull_second(delta_wide)
    returned = from_behind(grad_padded[:, :, :1], "space", -1)
    grad_hidden = jnp.concatenate(
        [grad_padded[:, :, 1:-1], grad_padded[:, :, -1:] + returned], axis=2
    )
    delta_one = (grad_hidden * leaky_slope(preact_one)).astype(jnp.bfloat16)
    inputs_wide = padded_in.astype(jnp.float32)

    def first_map(kernel):
        return strided_exact(inputs_wide, kernel, (0, 0))

    _, pull_first = jax.vjp(first_map, first_kernel.astype(jnp.float32))
    (first_local,) = pull_first(delta_one.astype(jnp.float32))
    flat_grad = second_gradient.reshape(-1)
    share = first_moment.shape[0]
    offset = lax.axis_index(("dp", "space")) * share
    total_second, first_gradient = lax.psum((flat_grad, first_local), ("dp", "space"))
    grad_share = lax.dynamic_slice_in_dim(total_second, offset, share, 0)
    new_first = BETA_FIRST * first_moment + (1.0 - BETA_FIRST) * grad_share
    new_second = BETA_SECOND * second_moment + (1.0 - BETA_SECOND) * grad_share * grad_share
    kernel_share = lax.dynamic_slice_in_dim(second_kernel.reshape(-1), offset, share, 0)
    updated_share = kernel_share - LEARN_RATE * new_first / (jnp.sqrt(new_second) + EPSILON)
    new_kernel = lax.all_gather(updated_share, ("dp", "space"), axis=0, tiled=True).reshape(
        second_kernel.shape
    )
    return (activations, first_gradient, new_kernel, new_first, new_second)


def solution(mesh):
    in_specs = (
        P("dp", None, "space", None, None),
        P(),
        P(),
        P("dp", None, "space", None, None),
        P(("dp", "space")),
        P(("dp", "space")),
    )
    out_specs = (
        P("dp", None, "space", None, None),
        P(),
        P(),
        P(("dp", "space")),
        P(("dp", "space")),
    )
    return jax.shard_map(shards, mesh=mesh, in_specs=in_specs, out_specs=out_specs, check_vma=False)
```

profile of v0, /device:TPU:0, one launch (start us, length us, event | category | flops | bytes accessed | tf_op | source)
XLA Modules:
  0.0 863.5 jit_solution(15912801684704176963)
XLA Ops:
  18.8 3.9 reshape.24
  22.7 19.7 %copy.66 = bf16[4,9,32,1,8,66]{4,0,5,2,1,3:T(4,128)(2,1)} copy(bf16[4,9,32,1,8,66]{5,4,2,1,0,3:T(8,128)(2,1)S(1)} %reshape.24) | data formatting | bytes 2433024 | tf_op jit(solution)/shard_map/conv_general_dilated | solution.py:21
  43.9 63.5 %compare_select_fusion = (f32[4,16,8,33,32]{4,2,3,1,0:T(8,128)}, bf16[4,16,8,33,32]{4,2,3,1,0:T(8,128)(2,1)S(1)}) fusion(pred[8,33]{0,1:T(8,128)(4,1)S(1)} %copy-done.12, bf16[3,3,3,4,32]{4,3,2,1,0:T(4,128)(2,1)S(1)} %copy-done, bf16[4,9,32,1,7,2]{4,0,5,2,1,3:T(4,128)(2,1)S(1)} %slice.35, bf16[4,9,32,1,8,66]{4,0,5,2,1,3:T(4,128)(2,1)} %copy.66), kind=kOutput, calls=%fused_computation.8 | convolution fusion | flops 121356288 | bytes 4499976 | tf_op jit(solution)/shard_map/conv_general_dilated | solution.py:21
  107.6 3.9 copy.90
  113.8 4.6 collective-permute-start.1
  118.4 24.8 %reshape.72 = bf16[4,16,1,264,32]{4,2,3,1,0:T(2,128)(2,1)} reshape(bf16[4,16,8,33,32]{4,3,2,1,0:T(8,128)(2,1)} %copy.90) | data formatting | bytes 2162688 | tf_op jit(solution)/shard_map/convert_element_type | solution.py:54
  143.2 11.1 %slice_bitcast_fusion = bf16[1,32,4,16,256]{1,0,4,3,2:T(2,128)(2,1)} fusion(bf16[4,16,1,264,32]{4,2,3,1,0:T(2,128)(2,1)} %reshape.72), kind=kLoop, calls=%fused_computation.12 | loop fusion | bytes 2097152 | tf_op jit(solution)/shard_map/convert_element_type | solution.py:54
  154.4 80.1 %copy.86 = bf16[1,4,9,32,512]{1,0,4,3,2:T(2,128)(2,1)} copy(bf16[1,4,9,32,512]{4,3,2,1,0:T(8,128)(2,1)S(1)} %copy-done.4) | data formatting | bytes 2359296 | tf_op jit(solution)/shard_map/concatenate | solution.py:52
  234.4 10.7 %copy.85 = f32[4,16,8,33,32]{3,2,4,1,0:T(8,128)} copy(f32[4,16,8,33,32]{4,2,3,1,0:T(8,128)} %get-tuple-element.25) | data formatting | bytes 4325376 | tf_op jit(solution)/shard_map/jit(_where)/select_n | solution.py:47
  245.2 7.4 reshape.52
  253.8 32.8 %pad_maximum_fusion = bf16[1,32,5,16,256]{1,0,4,3,2:T(2,128)(2,1)} fusion(bf16[1,32,4,16,256]{1,0,4,3,2:T(2,128)(2,1)} %slice_bitcast_fusion, bf16[1,32,1,16,256]{1,0,4,3,2:T(2,128)(2,1)S(1)} %copy.71), kind=kLoop, calls=%fused_computation.9 | loop fusion | flops 655360 | bytes 2621440 | tf_op jit(solution)/shard_map/concatenate | solution.py:56
  286.6 13.3 %copy.72 = bf16[1,32,5,16,256]{4,3,2,1,0:T(8,128)(2,1)S(1)} copy(bf16[1,32,5,16,256]{1,0,4,3,2:T(2,128)(2,1)} %pad_maximum_fusion) | data formatting | bytes 2621440 | tf_op jit(solution)/shard_map/concatenate | solution.py:56
  300.7 5.6 reshape.31
  306.3 10.2 %copy.74 = bf16[32,5,16,1,8,34]{0,4,5,2,1,3:T(8,128)(2,1)} copy(bf16[32,5,16,1,8,34]{5,4,2,1,0,3:T(8,128)(2,1)} %reshape.31) | data formatting | bytes 2785280 | tf_op jit(solution)/shard_map/conv_general_dilated | solution.py:21
  317.7 7.2 compare_select_fusion.1
  325.3 25.5 %fusion.22 = f32[3,3,3,32,64]{4,3,2,1,0:T(8,128)S(1)} fusion(bf16[1,32,5,16,256]{1,0,4,3,2:T(2,128)(2,1)S(1)} %bitcast.86, bf16[1,64,2,8,128]{1,3,4,2,0:T(8,128)(2,1)S(1)} %fusion.21), kind=kOutput, calls=%fused_computation.31 | convolution fusion | flops 216489984 | bytes 1794048 | tf_op jit(solution)/shard_map/transpose(jvp())/conv_general_dilated | solution.py:32
  351.0 5.3 broadcast_select_fusion
  362.3 8.3 copy.80
  370.6 5.9 reshape.50
  388.1 97.6 %all-reduce.4.cloned.1.call-done = f32[55296]{0:T(1024)} async-done(((f32[55296]{0:T(1024)}), f32[55296]{0:T(1024)}) %all-reduce.4.cloned.1.call-update) | async-done | bytes 221200 | tf_op jit(solution)/shard_map/psum | solution.py:85
  494.5 121.3 %all-reduce.6.cloned.1.call-done = f32[55296]{0:T(1024)} async-done(((f32[55296]{0:T(1024)}), f32[55296]{0:T(1024)}) %all-reduce.6.cloned.1.call-update) | async-done | bytes 221200
  621.7 18.4 %copy.87 = bf16[1,32,4,16,256]{1,0,4,3,2:T(2,128)(2,1)} copy(bf16[1,32,4,16,256]{4,1,3,2,0:T(8,128)(2,1)} %fusion.14) | data formatting | bytes 2097152 | tf_op jit(solution)/shard_map/convert_element_type | solution.py:74
  640.1 173.7 %fusion.46 = f32[3,3,3,4,32]{4,3,2,1,0:T(4,128)S(1)} fusion(bf16[1,4,9,32,512]{1,0,4,3,2:T(2,128)(2,1)} %copy.86, bf16[1,32,4,16,256]{1,0,4,3,2:T(2,128)(2,1)} %copy.87), kind=kOutput, calls=%fused_computation.62 | convolution fusion | flops 110742528 | bytes 2242048 | tf_op jit(solution)/shard_map/transpose(jvp())/conv_general_dilated | solution.py:32
  813.9 42.3 %psum.14 = f32[3,3,3,4,32]{4,3,2,1,0:T(4,128)} all-reduce(f32[3,3,3,4,32]{4,3,2,1,0:T(4,128)S(1)} %fusion.46), channel_id=1, replica_groups=mesh['dp'=4,'space'=8] {'dp','space'}, use_global_device_ids=true, to_apply=%region_0.1 | all-reduce | flops 3456 | bytes 27648 | tf_op jit(solution)/shard_map/psum | solution.py:85
  (81 shorter events, 51.3 us)
Async XLA Ops:
  7.2 36.8 %copy-start = (bf16[3,3,3,4,32]{4,3,2,1,0:T(4,128)(2,1)S(1)}, bf16[3,3,3,4,32]{4,3,2,1,0:T(4,128)(2,1)}, u32[]{:S(2)}) copy-start(bf16[3,3,3,4,32]{4,3,2,1,0:T(4,128)(2,1)} %param.7) | copy-start | bytes 20740
  7.2 478.5 %all-reduce.4.cloned.1.call-start = ((), (), s32[]{:S(2)}) async-start(), calls=%async_computation | async-start | bytes 442368 | tf_op jit(solution)/shard_map/psum | solution.py:85
  8.2 6.3 collective-permute-start
  15.8 1.1 copy-start.3
  22.7 21.2 %copy-start.12 = (pred[8,33]{0,1:T(8,128)(4,1)S(1)}, pred[8,33]{0,1:T(8,128)(4,1)}, u32[]{:S(2)}) copy-start(pred[8,33]{0,1:T(8,128)(4,1)} %constant.50) | copy-start | bytes 796
  113.8 138.8 %collective-permute-start.1 = (bf16[1,32,1,16,256]{4,3,2,1,0:T(8,128)(2,1)S(1)}, bf16[1,32,1,16,256]{4,3,2,1,0:T(8,128)(2,1)S(1)}, u32[]{:S(2)}, u32[]{:S(2)}) collective-permute-start(bf16[1,32,1,16,256]{4,3,2,1,0:T(8,128)(2,1)S(1)} %copy.68), channel_id=1, source_target_pairs={{0,1},{1,2},{2,3},{3,4},{4,5},{5,6},{6,7},{8,9},{9,10},{10,11},{11... | collective-permute-start | bytes 786440 | tf_op jit(solution)/shard_map/ppermute | solution.py:17
  143.2 11.1 %copy-start.4 = (bf16[1,4,9,32,512]{4,3,2,1,0:T(8,128)(2,1)S(1)}, bf16[1,4,9,32,512]{4,3,2,1,0:T(8,128)(2,1)}, u32[]{:S(2)}) copy-start(bf16[1,4,9,32,512]{4,3,2,1,0:T(8,128)(2,1)} %copy-done.3) | copy-start | bytes 3538948
  306.3 11.4 %copy-start.7 = (f32[3,3,3,32,64]{4,3,2,1,0:T(8,128)S(1)}, f32[3,3,3,32,64]{4,3,2,1,0:T(8,128)}, u32[]{:S(2)}) copy-start(f32[3,3,3,32,64]{4,3,2,1,0:T(8,128)} %param.8) | copy-start | bytes 663556
  306.3 11.4 %copy-start.13 = (pred[8,17]{0,1:T(8,128)(4,1)S(1)}, pred[8,17]{0,1:T(8,128)(4,1)}, u32[]{:S(2)}) copy-start(pred[8,17]{0,1:T(8,128)(4,1)} %constant.49) | copy-start | bytes 412
  316.4 8.8 %slice-start = ((s8[10485760]{0:T(1024)(128)(4,1)}), s8[4194304]{0:T(1024)(128)(4,1)S(1)}, s32[]{:S(2)}) async-start(s8[10485760]{0:T(1024)(128)(4,1)} %bitcast.85), calls=%async_computation.2 | async-start | bytes 8388608
  317.7 7.5 copy-start.5
  317.7 7.6 slice-start.1
  317.7 7.6 slice-start.2
  325.3 25.7 %copy-start.8 = (f32[3,3,3,32,64]{4,3,2,1,0:T(8,128)S(1)}, f32[3,3,3,32,64]{4,3,2,1,0:T(8,128)}, u32[]{:S(2)}) copy-start(f32[3,3,3,32,64]{4,3,2,1,0:T(8,128)} %param.8) | copy-start | bytes 663556
  325.3 25.7 %copy-start.11 = (pred[8,34]{0,1:T(8,128)(4,1)S(1)}, pred[8,34]{0,1:T(8,128)(4,1)}, u32[]{:S(2)}) copy-start(pred[8,34]{0,1:T(8,128)(4,1)} %constant.51) | copy-start | bytes 820
  362.3 253.5 %all-reduce.6.cloned.1.call-start = ((), (), s32[]{:S(2)}) async-start(), calls=%async_computation.1 | async-start | bytes 442368
  376.5 109.2 %copy-start.9 = (f32[1728]{0:T(1024)S(1)}, f32[1728]{0:T(1024)}, u32[]{:S(2)}) copy-start(f32[1728]{0:T(1024)} %param.10) | copy-start | bytes 20740
  376.5 109.2 %copy-start.10 = (f32[1728]{0:T(1024)S(1)}, f32[1728]{0:T(1024)}, u32[]{:S(2)}) copy-start(f32[1728]{0:T(1024)} %param.11) | copy-start | bytes 20740
  382.8 234.8 %collective-permute-start.2 = (f32[1,32,1,16,256]{4,1,3,2,0:T(8,128)}, f32[1,32,1,16,256]{4,1,3,2,0:T(8,128)}, u32[]{:S(2)}, u32[]{:S(2)}) collective-permute-start(f32[1,32,1,16,256]{4,1,3,2,0:T(8,128)} %slice_bitcast_fusion.4), channel_id=1, source_target_pairs={{1,0},{2,1},{3,2},{4,3},{5,4},{6,5},{7,6},{9,8},{10,9},{11,10},{12... | collective-permute-start | bytes 1572872 | tf_op jit(solution)/shard_map/ppermute | solution.py:17
  487.2 0.7 copy-start.6
  491.5 127.4 %copy-start.2 = (f32[4,16,1,264,32]{3,4,1,0,2:T(8,128)S(1)}, f32[4,16,1,264,32]{3,4,1,0,2:T(8,128)}, u32[]{:S(2)}) copy-start(f32[4,16,1,264,32]{3,4,1,0,2:T(8,128)} %reshape.52) | copy-start | bytes 6488068
  640.1 216.0 %copy-start.1 = (bf16[3,3,3,4,32]{4,3,2,1,0:T(4,128)(2,1)S(1)}, bf16[3,3,3,4,32]{4,3,2,1,0:T(4,128)(2,1)}, u32[]{:S(2)}) copy-start(bf16[3,3,3,4,32]{4,3,2,1,0:T(4,128)(2,1)} %param.7) | copy-start | bytes 20740
Sparse Core Ops, SparseCore 0:
  362.4 123.2 all-reduce.3
  491.8 123.9 all-reduce.5
where the time goes:
time: 877 us; the launch traced here: 863 us
  matrix products  275 us (31%)
  local copies, waits for them, and re-layouts  265 us (30%)
  waiting for transfers between devices  219 us (25%)
  blocking collectives  42.3 us (5%)
  other arithmetic  38.4 us (4%)
  between operations  14.9 us (2%)
    conv_general_dilated x3, matrix products, strided_exact(): lax.conv_general_dilated(inputs, kernel, (2, 2, 2), [depth_pad, (1, 1), (...  205 us
    unnamed x3, waiting for transfers between devices  121 us
    psum x1, waiting for transfers between devices, shards(): lax.psum((flat_grad, first_local), ('dp', 'space'))  97.6 us
    concatenate x3, local copies, waits for them, and re-layouts, shards(): padded_in = jnp.concatenate([lower_plane, volumes], axis=2)  83.2 us
    conv_general_dilated x2, matrix products, strided(): lax.conv_general_dilated(inputs, kernel, (2, 2, 2), [(0, 0), (1, 1), (1,...  70.8 us
    psum x1, blocking collectives, shards(): lax.psum((flat_grad, first_local), ('dp', 'space'))  42.3 us
    conv_general_dilated x6, local copies, waits for them, and re-layouts, strided(): lax.conv_general_dilated(inputs, kernel, (2, 2, 2), [(0, 0), (1, 1), (1,...  42.1 us
    convert_element_type x6, local copies, waits for them, and re-layouts, shards(): hidden = leaky(preact_one).astype(jnp.bfloat16)  42 us
  transfers between devices with their start and end apart: 5, of which 2 were waited for; matrix products, arithmetic and copies ran while one was open for 20% of the time, Pallas kernels for 0%

commit v1 on v0

--- a/solution.py
+++ b/solution.py
@@ -82,7 +82,7 @@
     flat_grad = second_gradient.reshape(-1)
     share = first_moment.shape[0]
     offset = lax.axis_index(("dp", "space")) * share
-    total_second, first_gradient = lax.psum((flat_grad, first_local), ("dp", "space"))
+    total_second, first_gradient = lax.psum(lax.psum((flat_grad, first_local), "space"), "dp")
     grad_share = lax.dynamic_slice_in_dim(total_second, offset, share, 0)
     new_first = BETA_FIRST * first_moment + (1.0 - BETA_FIRST) * grad_share
     new_second = BETA_SECOND * second_moment + (1.0 - BETA_SECOND) * grad_share * grad_share

time: 877 us -> 844 us (0.962)
  waiting for transfers between devices: 219 us -> 178 us
    psum x1 -> x2, waiting for transfers between devices: 97.6 us -> 57.5 us  [the longest x1 44.5 us: shards(): lax.psum(lax.psum((flat_grad, first_local), 'space'), 'dp')]
    psum x1 -> x2, blocking collectives: 42.3 us -> 45.7 us  [the longest x1 28.3 us: shards(): lax.psum((flat_grad, first_local), 'space')]
    unnamed x3 -> x4, waiting for transfers between devices: 121 us -> 121 us
  transfers between devices with their start and end apart: 5 -> 6, of which waited for: 2 -> 3; matrix products, arithmetic and copies ran while one was open for 20% -> 22% of each run, Pallas kernels for 0% -> 0%
where the time goes in v1:
time: 844 us; the launch traced here: 831 us
  matrix products  275 us (33%)
  local copies, waits for them, and re-layouts  270 us (32%)
  waiting for transfers between devices  178 us (21%)
  blocking collectives  45.7 us (5%)
  other arithmetic  38.4 us (5%)
  between operations  14.7 us (2%)
  starting transfers between devices  8.62 us (1%)
    conv_general_dilated x3, matrix products, strided_exact(): lax.conv_general_dilated(inputs, kernel, (2, 2, 2), [depth_pad, (1, 1), (...  204 us
    unnamed x4, waiting for transfers between devices  121 us
    concatenate x3, local copies, waits for them, and re-layouts, shards(): padded_in = jnp.concatenate([lower_plane, volumes], axis=2)  82 us
    conv_general_dilated x2, matrix products, strided(): lax.conv_general_dilated(inputs, kernel, (2, 2, 2), [(0, 0), (1, 1), (1,...  70.8 us
    psum x1, waiting for transfers between devices, shards(): lax.psum(lax.psum((flat_grad, first_local), 'space'), 'dp')  44.5 us
    conv_general_dilated x6, local copies, waits for them, and re-layouts, strided(): lax.conv_general_dilated(inputs, kernel, (2, 2, 2), [(0, 0), (1, 1), (1,...  42.1 us
    convert_element_type x6, local copies, waits for them, and re-layouts, shards(): hidden = leaky(preact_one).astype(jnp.bfloat16)  42.1 us
    concatenate x1, other arithmetic, shards(): padded_hidden = jnp.concatenate([lower_hidden, hidden], axis=2)  32.8 us
  transfers between devices with their start and end apart: 6, of which 3 were waited for; matrix products, arithmetic and copies ran while one was open for 22% of the time, Pallas kernels for 0%

profile of v1, /device:TPU:0, one launch (start us, length us, event | category | flops | bytes accessed | tf_op | source)
XLA Modules:
  0.0 830.5 jit_solution(1730301900089737953)
XLA Ops:
  22.7 19.7 %copy.66 = bf16[4,9,32,1,8,66]{4,0,5,2,1,3:T(4,128)(2,1)} copy(bf16[4,9,32,1,8,66]{5,4,2,1,0,3:T(8,128)(2,1)S(1)} %reshape.24) | data formatting | bytes 2433024 | tf_op jit(solution)/shard_map/conv_general_dilated | solution.py:21
  44.0 63.6 %compare_select_fusion = (f32[4,16,8,33,32]{4,2,3,1,0:T(8,128)}, bf16[4,16,8,33,32]{4,2,3,1,0:T(8,128)(2,1)S(1)}) fusion(pred[8,33]{0,1:T(8,128)(4,1)S(1)} %copy-done.14, bf16[3,3,3,4,32]{4,3,2,1,0:T(4,128)(2,1)S(1)} %copy-done, bf16[4,9,32,1,7,2]{4,0,5,2,1,3:T(4,128)(2,1)S(1)} %slice.35, bf16[4,9,32,1,8,66]{4,0,5,2,1,3:T(4,128)(2,1)} %copy.66), kind=kOutput, calls=%fused_computation.8 | convolution fusion | flops 121356288 | bytes 4499976 | tf_op jit(solution)/shard_map/conv_general_dilated | solution.py:21
  118.5 24.8 %reshape.72 = bf16[4,16,1,264,32]{4,2,3,1,0:T(2,128)(2,1)} reshape(bf16[4,16,8,33,32]{4,3,2,1,0:T(8,128)(2,1)} %copy.90) | data formatting | bytes 2162688 | tf_op jit(solution)/shard_map/convert_element_type | solution.py:54
  143.3 11.1 %slice_bitcast_fusion = bf16[1,32,4,16,256]{1,0,4,3,2:T(2,128)(2,1)} fusion(bf16[4,16,1,264,32]{4,2,3,1,0:T(2,128)(2,1)} %reshape.72), kind=kLoop, calls=%fused_computation.12 | loop fusion | bytes 2097152 | tf_op jit(solution)/shard_map/convert_element_type | solution.py:54
  154.5 78.9 %copy.86 = bf16[1,4,9,32,512]{1,0,4,3,2:T(2,128)(2,1)} copy(bf16[1,4,9,32,512]{4,3,2,1,0:T(8,128)(2,1)S(1)} %copy-done.5) | data formatting | bytes 2359296 | tf_op jit(solution)/shard_map/concatenate | solution.py:52
  233.3 10.7 %copy.85 = f32[4,16,8,33,32]{3,2,4,1,0:T(8,128)} copy(f32[4,16,8,33,32]{4,2,3,1,0:T(8,128)} %get-tuple-element.25) | data formatting | bytes 4325376 | tf_op jit(solution)/shard_map/jit(_where)/select_n | solution.py:47
  244.0 7.4 reshape.52
  252.7 32.8 %pad_maximum_fusion = bf16[1,32,5,16,256]{1,0,4,3,2:T(2,128)(2,1)} fusion(bf16[1,32,4,16,256]{1,0,4,3,2:T(2,128)(2,1)} %slice_bitcast_fusion, bf16[1,32,1,16,256]{1,0,4,3,2:T(2,128)(2,1)S(1)} %copy.71), kind=kLoop, calls=%fused_computation.9 | loop fusion | flops 655360 | bytes 2621440 | tf_op jit(solution)/shard_map/concatenate | solution.py:56
  285.5 13.3 %copy.72 = bf16[1,32,5,16,256]{4,3,2,1,0:T(8,128)(2,1)S(1)} copy(bf16[1,32,5,16,256]{1,0,4,3,2:T(2,128)(2,1)} %pad_maximum_fusion) | data formatting | bytes 2621440 | tf_op jit(solution)/shard_map/concatenate | solution.py:56
  299.6 5.6 reshape.31
  305.2 10.1 %copy.74 = bf16[32,5,16,1,8,34]{0,4,5,2,1,3:T(8,128)(2,1)} copy(bf16[32,5,16,1,8,34]{5,4,2,1,0,3:T(8,128)(2,1)} %reshape.31) | data formatting | bytes 2785280 | tf_op jit(solution)/shard_map/conv_general_dilated | solution.py:21
  316.6 7.2 compare_select_fusion.1
  324.2 25.2 %fusion.22 = f32[3,3,3,32,64]{4,3,2,1,0:T(8,128)S(1)} fusion(bf16[1,32,5,16,256]{1,0,4,3,2:T(2,128)(2,1)S(1)} %bitcast.86, bf16[1,64,2,8,128]{1,3,4,2,0:T(8,128)(2,1)S(1)} %fusion.21), kind=kOutput, calls=%fused_computation.31 | convolution fusion | flops 216489984 | bytes 1794048 | tf_op jit(solution)/shard_map/transpose(jvp())/conv_general_dilated | solution.py:32
  350.8 5.5 broadcast_select_fusion
  368.4 6.1 slice.43
  374.5 8.3 copy.80
  382.9 6.0 reshape.50
  390.1 13.0 %all-reduce.5.cloned.1.call-done = f32[55296]{0:T(1024)} async-done(((f32[55296]{0:T(1024)}), f32[55296]{0:T(1024)}) %all-reduce.5.cloned.1.call-update) | async-done | bytes 221200 | tf_op jit(solution)/shard_map/psum | solution.py:85
  406.0 44.5 %all-reduce.7.cloned.1.call-done = f32[55296]{0:T(1024)} async-done(((f32[55296]{0:T(1024)}), f32[55296]{0:T(1024)}) %all-reduce.7.cloned.1.call-update) | async-done | bytes 221200 | tf_op jit(solution)/shard_map/psum | solution.py:85
  459.1 120.7 %all-reduce.9.cloned.1.call-done = f32[55296]{0:T(1024)} async-done(((f32[55296]{0:T(1024)}), f32[55296]{0:T(1024)}) %all-reduce.9.cloned.1.call-update) | async-done | bytes 221200
  585.6 18.4 %copy.87 = bf16[1,32,4,16,256]{1,0,4,3,2:T(2,128)(2,1)} copy(bf16[1,32,4,16,256]{4,1,3,2,0:T(8,128)(2,1)} %fusion.14) | data formatting | bytes 2097152 | tf_op jit(solution)/shard_map/convert_element_type | solution.py:74
  604.0 173.7 %fusion.46 = f32[3,3,3,4,32]{4,3,2,1,0:T(4,128)S(1)} fusion(bf16[1,4,9,32,512]{1,0,4,3,2:T(2,128)(2,1)} %copy.86, bf16[1,32,4,16,256]{1,0,4,3,2:T(2,128)(2,1)} %copy.87), kind=kOutput, calls=%fused_computation.62 | convolution fusion | flops 110742528 | bytes 2242048 | tf_op jit(solution)/shard_map/transpose(jvp())/conv_general_dilated | solution.py:32
  777.7 28.3 %psum.28 = f32[3,3,3,4,32]{4,3,2,1,0:T(4,128)S(1)} all-reduce(f32[3,3,3,4,32]{4,3,2,1,0:T(4,128)S(1)} %fusion.46), channel_id=1, replica_groups=mesh['dp'=4,'space'=8] {'space'}, use_global_device_ids=true, to_apply=%region_0.1 | all-reduce | flops 3456 | bytes 27648 | tf_op jit(solution)/shard_map/psum | solution.py:85
  806.0 17.5 %psum.29 = f32[3,3,3,4,32]{4,3,2,1,0:T(4,128)} all-reduce(f32[3,3,3,4,32]{4,3,2,1,0:T(4,128)S(1)} %psum.28), channel_id=1, replica_groups=mesh['dp'=4,'space'=8] {'dp'}, use_global_device_ids=true, to_apply=%region_1.2 | all-reduce | flops 3456 | bytes 27648 | tf_op jit(solution)/shard_map/psum | solution.py:85
  (89 shorter events, 63.4 us)
Async XLA Ops:
  7.2 36.8 %copy-start = (bf16[3,3,3,4,32]{4,3,2,1,0:T(4,128)(2,1)S(1)}, bf16[3,3,3,4,32]{4,3,2,1,0:T(4,128)(2,1)}, u32[]{:S(2)}) copy-start(bf16[3,3,3,4,32]{4,3,2,1,0:T(4,128)(2,1)} %param.7) | copy-start | bytes 20740
  7.2 395.9 %all-reduce.5.cloned.1.call-start = ((), (), s32[]{:S(2)}) async-start(), calls=%async_computation | async-start | bytes 442368 | tf_op jit(solution)/shard_map/psum | solution.py:85
  8.2 6.4 collective-permute-start
  15.8 1.1 copy-start.4
  22.7 21.3 %copy-start.14 = (pred[8,33]{0,1:T(8,128)(4,1)S(1)}, pred[8,33]{0,1:T(8,128)(4,1)}, u32[]{:S(2)}) copy-start(pred[8,33]{0,1:T(8,128)(4,1)} %constant.50) | copy-start | bytes 796
  113.9 137.6 %collective-permute-start.1 = (bf16[1,32,1,16,256]{4,3,2,1,0:T(8,128)(2,1)S(1)}, bf16[1,32,1,16,256]{4,3,2,1,0:T(8,128)(2,1)S(1)}, u32[]{:S(2)}, u32[]{:S(2)}) collective-permute-start(bf16[1,32,1,16,256]{4,3,2,1,0:T(8,128)(2,1)S(1)} %copy.68), channel_id=1, source_target_pairs={{0,1},{1,2},{2,3},{3,4},{4,5},{5,6},{6,7},{8,9},{9,10},{10,11},{11... | collective-permute-start | bytes 786440 | tf_op jit(solution)/shard_map/ppermute | solution.py:17
  143.3 11.1 %copy-start.5 = (bf16[1,4,9,32,512]{4,3,2,1,0:T(8,128)(2,1)S(1)}, bf16[1,4,9,32,512]{4,3,2,1,0:T(8,128)(2,1)}, u32[]{:S(2)}) copy-start(bf16[1,4,9,32,512]{4,3,2,1,0:T(8,128)(2,1)} %copy-done.4) | copy-start | bytes 3538948
  305.2 11.4 %copy-start.9 = (f32[3,3,3,32,64]{4,3,2,1,0:T(8,128)S(1)}, f32[3,3,3,32,64]{4,3,2,1,0:T(8,128)}, u32[]{:S(2)}) copy-start(f32[3,3,3,32,64]{4,3,2,1,0:T(8,128)} %param.8) | copy-start | bytes 663556
  305.2 11.4 %copy-start.15 = (pred[8,17]{0,1:T(8,128)(4,1)S(1)}, pred[8,17]{0,1:T(8,128)(4,1)}, u32[]{:S(2)}) copy-start(pred[8,17]{0,1:T(8,128)(4,1)} %constant.49) | copy-start | bytes 412
  315.3 8.8 %slice-start = ((s8[10485760]{0:T(1024)(128)(4,1)}), s8[4194304]{0:T(1024)(128)(4,1)S(1)}, s32[]{:S(2)}) async-start(s8[10485760]{0:T(1024)(128)(4,1)} %bitcast.85), calls=%async_computation.3 | async-start | bytes 8388608
  316.5 7.4 copy-start.6
  316.6 7.5 slice-start.1
  316.6 7.5 slice-start.2
  324.1 26.6 %copy-start.10 = (f32[3,3,3,32,64]{4,3,2,1,0:T(8,128)S(1)}, f32[3,3,3,32,64]{4,3,2,1,0:T(8,128)}, u32[]{:S(2)}) copy-start(f32[3,3,3,32,64]{4,3,2,1,0:T(8,128)} %param.8) | copy-start | bytes 663556
  324.1 26.6 %copy-start.13 = (pred[8,34]{0,1:T(8,128)(4,1)S(1)}, pred[8,34]{0,1:T(8,128)(4,1)}, u32[]{:S(2)}) copy-start(pred[8,34]{0,1:T(8,128)(4,1)} %constant.51) | copy-start | bytes 820
  350.2 100.3 %all-reduce.7.cloned.1.call-start = ((), (), s32[]{:S(2)}) async-start(), calls=%async_computation.1 | async-start | bytes 442368 | tf_op jit(solution)/shard_map/psum | solution.py:85
  356.3 4.2 copy-start.2
  382.8 23.1 %copy-start.8 = (bf16[2,8,8,17,64]{4,2,3,1,0:T(8,128)(2,1)S(1)}, bf16[2,8,8,17,64]{4,2,3,1,0:T(8,128)(2,1)}, u32[]{:S(2)}) copy-start(bf16[2,8,8,17,64]{4,2,3,1,0:T(8,128)(2,1)} %get-tuple-element.28) | copy-start | bytes 835588
  382.8 67.7 %copy-start.11 = (f32[1728]{0:T(1024)S(1)}, f32[1728]{0:T(1024)}, u32[]{:S(2)}) copy-start(f32[1728]{0:T(1024)} %param.10) | copy-start | bytes 20740
  382.9 67.7 %copy-start.12 = (f32[1728]{0:T(1024)S(1)}, f32[1728]{0:T(1024)}, u32[]{:S(2)}) copy-start(f32[1728]{0:T(1024)} %param.11) | copy-start | bytes 20740
  388.8 192.7 %collective-permute-start.2 = (f32[1,32,1,16,256]{4,1,3,2,0:T(8,128)}, f32[1,32,1,16,256]{4,1,3,2,0:T(8,128)}, u32[]{:S(2)}, u32[]{:S(2)}) collective-permute-start(f32[1,32,1,16,256]{4,1,3,2,0:T(8,128)} %slice_bitcast_fusion.4), channel_id=1, source_target_pairs={{1,0},{2,1},{3,2},{4,3},{5,4},{6,5},{7,6},{9,8},{10,9},{11,10},{12... | collective-permute-start | bytes 1572872 | tf_op jit(solution)/shard_map/ppermute | solution.py:17
  403.1 176.6 %all-reduce.9.cloned.1.call-start = ((), (), s32[]{:S(2)}) async-start(), calls=%async_computation.2 | async-start | bytes 442368
  456.1 126.7 %copy-start.3 = (f32[4,16,1,264,32]{3,4,1,0,2:T(8,128)S(1)}, f32[4,16,1,264,32]{3,4,1,0,2:T(8,128)}, u32[]{:S(2)}) copy-start(f32[4,16,1,264,32]{3,4,1,0,2:T(8,128)} %reshape.52) | copy-start | bytes 6488068
  604.0 219.5 %copy-start.1 = (bf16[3,3,3,4,32]{4,3,2,1,0:T(4,128)(2,1)S(1)}, bf16[3,3,3,4,32]{4,3,2,1,0:T(4,128)(2,1)}, u32[]{:S(2)}) copy-start(bf16[3,3,3,4,32]{4,3,2,1,0:T(4,128)(2,1)} %param.7) | copy-start | bytes 20740
  (1 other events, 0.7 us)
Sparse Core Ops, SparseCore 0:
  350.3 52.7 all-reduce.4
  406.3 44.1 all-reduce.6
  456.7 123.0 all-reduce.8
